TPU v7x, 512 devices: a whole 4x8x8 slice. The times are simulated.
512 devices in a mesh: dp: 16 (over z, core), mp: 32 (over y, x).
Axes of the slice: x: 4, y: 8, z: 8, core: 2. Of those that a mesh axis runs over, the one named last changes fastest.
Arguments:
- inputs: bfloat16 [32768, 4096], P('dp', 'mp'), may hold values from -6 to 6
- out_grad: bfloat16 [32768, 4096], P('dp', 'mp'), may hold values from -6 to 6
- mean_state: float32 [6, 64, 64, 64], P(None, 'mp', 'dp'), may hold values from -0.75 to 0.75
- hess_state: float32 [6, 64, 64, 64], P(None, 'mp', 'dp'), may hold values from 2 to 20
- grad_state: float32 [6, 64, 64, 64], P(None, 'mp', 'dp'), may hold values from -1.8 to 1.8
- noise_draw: float32 [16, 6, 64, 64, 64], P('dp', None, 'mp'), may hold values from -6 to 6
Outputs:
- new_mean: float32 [6, 64, 64, 64], P(None, 'mp', 'dp')
- new_hess: float32 [6, 64, 64, 64], P(None, 'mp', 'dp')
- new_grad: float32 [6, 64, 64, 64], P(None, 'mp', 'dp')
All inputs are finite; a program needn't handle non-finite values.
Results may differ from a plain program's by a relative error of at most 0.0018.
Values may be sent and summed in bfloat16 or wider, within the bound.
No kernel may reach another device: no remote copies, remote signals or barrier semaphores. Data moves between devices by JAX's collectives and lax.ppermute only.
A program may use at most 64 MiB of HBM per device.

v0:
```python
import jax
import jax.numpy as jnp
from jax import lax
from jax.sharding import PartitionSpec as P

LAMBDA_SIZE = 100.0
DELTA_DAMP = 0.001
BETA_GRAD = 0.9
BETA_HESS = 0.9
STEP_RATE = 1.0
REDUCE_MODE = "a2a"


def bdot(form, left, right):
    return jnp.einsum(form, left, right, preferred_element_type=jnp.float32)


def silu_slope(value):
    sigm = jax.nn.sigmoid(value)
    return sigm * (1.0 + value * (1.0 - sigm))


def gather_rows(stacked, groups):
    moved = jnp.moveaxis(stacked, 3, 0)
    full = lax.all_gather(moved, "dp", axis=0, tiled=True)
    return jnp.moveaxis(full, 0, 3)


def scatter_rows(stacked, groups):
    s, f, b, r, w = stacked.shape
    split = stacked.reshape(s, f, b, groups, r // groups, w)
    split = jnp.moveaxis(split, 3, 0)
    if REDUCE_MODE == "a2a":
        got = lax.all_to_all(split, "dp", split_axis=0, concat_axis=0, tiled=True)
        summed = jnp.sum(got, axis=0)
    else:
        summed = lax.psum_scatter(split, "dp", scatter_dimension=0, tiled=False)
    return summed


def per_device(inputs, out_grad, mean_state, hess_state, grad_state, noise_draw):
    tokens = inputs.shape[0]
    local_blocks = mean_state.shape[1]
    width = mean_state.shape[3]
    groups = lax.axis_size("dp")
    scale = tokens ** (-0.5)
    full = gather_rows(jnp.stack([mean_state, hess_state]), groups)
    full_mean, full_hess = (full[0], full[1])
    spread = jnp.sqrt(LAMBDA_SIZE * (full_hess + DELTA_DAMP))
    noise = noise_draw[0]
    sampled = (full_mean + noise / spread).astype(jnp.bfloat16)
    in_rows = inputs.reshape(tokens, local_blocks, width)
    grad_rows = out_grad.reshape(tokens, local_blocks, width)
    y_left = bdot("tbr,brc->tcb", in_rows, sampled[0]).astype(jnp.bfloat16)
    y_right = bdot("tbr,brc->tcb", in_rows, sampled[2]).astype(jnp.bfloat16)
    back_outer = bdot("tjc,jic->tij", grad_rows, sampled[5]).astype(jnp.bfloat16)
    first = lax.all_to_all(
        jnp.stack([y_left, y_right, back_outer], axis=1),
        "mp",
        split_axis=2,
        concat_axis=3,
        tiled=True,
    )
    perm_left, perm_right, back_hidden = (first[:, 0], first[:, 1], first[:, 2])
    u_left = bdot("tji,jic->tjc", perm_left, sampled[1])
    u_right = bdot("tji,jic->tjc", perm_right, sampled[3])
    hidden = (jax.nn.silu(u_left) * u_right).astype(jnp.bfloat16)
    outer = bdot("tbr,brc->tcb", hidden, sampled[4]).astype(jnp.bfloat16)
    grad_four = bdot("tbr,tbc->brc", hidden, back_hidden) * scale
    d_hidden = bdot("tbc,brc->tbr", back_hidden, sampled[4])
    gate_grad = (d_hidden * u_right * silu_slope(u_left)).astype(jnp.bfloat16)
    value_grad = (d_hidden * jax.nn.silu(u_left)).astype(jnp.bfloat16)
    grad_one = bdot("tji,tjc->jic", perm_left, gate_grad) * scale
    grad_three = bdot("tji,tjc->jic", perm_right, value_grad) * scale
    back_left = bdot("tjc,jic->tij", gate_grad, sampled[1]).astype(jnp.bfloat16)
    back_right = bdot("tjc,jic->tij", value_grad, sampled[3]).astype(jnp.bfloat16)
    second = lax.all_to_all(
        jnp.stack([outer, back_left, back_right], axis=1),
        "mp",
        split_axis=2,
        concat_axis=3,
        tiled=True,
    )
    mixed_rows, rows_left, rows_right = (second[:, 0], second[:, 1], second[:, 2])
    grad_five = bdot("tji,tjc->jic", mixed_rows, grad_rows) * scale
    grad_zero = bdot("tbr,tbc->brc", in_rows, rows_left) * scale
    grad_two = bdot("tbr,tbc->brc", in_rows, rows_right) * scale
    all_grads = jnp.stack([grad_zero, grad_one, grad_two, grad_three, grad_four, grad_five])
    sums = scatter_rows(jnp.stack([all_grads, all_grads * noise * spread]), groups)
    grad_avg = sums[0] / groups
    hess_avg = sums[1] / groups
    new_grad = BETA_GRAD * grad_state + (1.0 - BETA_GRAD) * grad_avg
    new_hess = (
        BETA_HESS * hess_state
        + (1.0 - BETA_HESS) * hess_avg
        + 0.5 * (1.0 - BETA_HESS) ** 2 * (hess_state - hess_avg) ** 2 / (hess_state + DELTA_DAMP)
    )
    new_mean = mean_state - STEP_RATE * (new_grad + DELTA_DAMP * mean_state) / (
        new_hess + DELTA_DAMP
    )
    return (new_mean, new_hess, new_grad)


def solution(mesh):
    return jax.shard_map(
        per_device,
        mesh=mesh,
        in_specs=(
            P("dp", "mp"),
            P("dp", "mp"),
            P(None, "mp", "dp", None),
            P(None, "mp", "dp", None),
            P(None, "mp", "dp", None),
            P("dp", None, "mp", None, None),
        ),
        out_specs=(P(None, "mp", "dp", None), P(None, "mp", "dp", None), P(None, "mp", "dp", None)),
        check_vma=False,
    )
```

profile of v0, /device:TPU:1, one launch (start us, length us, event | category | flops | bytes accessed | tf_op | source)
XLA Modules:
  0.0 176.5 jit_solution(16778097129029193267)
XLA Ops:
  0.6 0.0 copy-start.9
  0.6 0.8 pad_maximum_fusion.2
  1.5 0.0 copy-start.5
  1.5 26.8 %all_gather.3 = f32[64,2,6,2,64]{4,3,2,1,0:T(2,128)S(1)} all-gather(f32[4,2,6,2,64]{4,3,2,1,0:T(2,128)S(1)} %bitcast.183), channel_id=1, replica_groups=mesh['dp'=16,'mp'=32] {'dp'}, dimensions={0}, use_global_device_ids=true | all-gather | bytes 417792 | tf_op jit(solution)/shard_map/all_gather | solution.py:25
  28.3 0.4 copy.61
  28.7 0.0 copy-done.9
  28.7 0.2 copy.62
  28.9 0.0 copy-done.5
  28.9 0.2 copy.63
  29.1 0.1 fusion.8
  29.2 0.3 fusion
  29.5 0.3 fusion.1
  29.8 1.2 copy.64
  31.1 0.0 copy-start.2
  31.1 0.3 fusion.2
  31.4 0.2 pad_maximum_fusion
  31.6 0.3 copy-done.2
  31.9 1.6 copy.66
  33.5 48.9 %all_to_all.41 = bf16[2048,3,64,2]{0,3,1,2:T(2,128)(2,1)S(1)} all-to-all(bf16[2048,3,64,2]{0,3,1,2:T(2,128)(2,1)S(1)} %copy.66), channel_id=1, replica_groups=mesh['dp'=16,'mp'=32] {'mp'}, dimensions={2} | all-to-all | bytes 3145728 | tf_op jit(solution)/shard_map/all_to_all | solution.py:57
  82.4 1.3 copy.102
  83.6 2.0 %all_to_all.32 = bf16[2048,3,2,64]{0,3,2,1:T(8,128)(2,1)} reshape(bf16[2048,3,2,32,2]{0,4,3,2,1:T(2,128)(2,1)S(1)} %bitcast.163) | data formatting | bytes 3145728 | tf_op jit(solution)/shard_map/all_to_all | solution.py:57
  85.7 1.5 convolution_bitcast_fusion
  87.2 0.1 copy-done
  87.2 0.3 convolution_bitcast_fusion.2
  87.5 0.6 multiply_convert_fusion.2
  88.1 0.0 copy-start.8
  88.2 0.3 fusion.3
  88.5 0.3 fusion.4
  88.8 0.1 copy-done.8
  88.9 0.2 copy-done.7
  89.1 0.3 fusion.5
  89.5 0.2 pad_maximum_fusion.1
  89.7 1.6 copy.71
  91.3 42.3 %all_to_all.42 = bf16[2048,3,64,2]{0,3,1,2:T(2,128)(2,1)S(1)} all-to-all(bf16[2048,3,64,2]{0,3,1,2:T(2,128)(2,1)S(1)} %copy.71), channel_id=1, replica_groups=mesh['dp'=16,'mp'=32] {'mp'}, dimensions={2} | all-to-all | bytes 3145728 | tf_op jit(solution)/shard_map/all_to_all | solution.py:77
  133.6 1.3 copy.101
  134.9 2.0 %all_to_all.36 = bf16[2048,3,2,64]{0,3,2,1:T(8,128)(2,1)} reshape(bf16[2048,3,2,32,2]{0,4,3,2,1:T(2,128)(2,1)S(1)} %bitcast.165) | data formatting | bytes 3145728 | tf_op jit(solution)/shard_map/all_to_all | solution.py:77
  136.9 1.4 convolution_multiply_fusion.5
  138.4 1.3 convolution_multiply_fusion.3
  139.7 0.1 copy.83
  139.8 0.6 constant_dynamic-update-slice_fusion.7
  140.4 2.0 %bitcast_dynamic-update-slice_fusion.3 = (f32[1,6,2,64,64]{3,4,2,1,0:T(8,128)}, f32[2,64,64]{1,2,0:T(8,128)S(1)}) fusion(f32[1,6,2,64,64]{3,4,2,1,0:T(8,128)} %constant_dynamic-update-slice_fusion.7, bf16[2048,2,64]{0,2,1:T(8,128)(2,1)} %copy-done.8, bf16[2048,3,2,64]{0,3,2,1:T(8,128)(2,1)S(1)} %copy-done.1), kind=kOutput, calls=%fused_computation.45 | convolution fusion | flops 33562624 | bytes 1146880 | tf_op jit(solution)/shard_map/tji,tjc->jic/dot_general | solution.py:15
  142.4 0.1 copy.75
  142.5 0.6 constant_dynamic-update-slice_fusion.5
  143.1 0.1 copy.84
  143.2 0.6 constant_dynamic-update-slice_fusion.6
  143.8 1.9 %bitcast_dynamic-update-slice_fusion.2 = (f32[1,6,2,64,64]{3,4,2,1,0:T(8,128)}, f32[2,64,64]{1,2,0:T(8,128)S(1)}) fusion(f32[1,6,2,64,64]{3,4,2,1,0:T(8,128)} %constant_dynamic-update-slice_fusion.6, bf16[2048,2,64]{0,2,1:T(8,128)(2,1)} %copy-done.7, bf16[2048,3,2,64]{0,3,2,1:T(8,128)(2,1)S(1)} %copy-done.1), kind=kOutput, calls=%fused_computation.44 | convolution fusion | flops 33562624 | bytes 1146880 | tf_op jit(solution)/shard_map/tji,tjc->jic/dot_general | solution.py:15
  145.8 0.1 copy.78
  145.8 1.9 %bitcast_dynamic-update-slice_fusion.1 = (f32[1,6,2,64,64]{3,4,2,1,0:T(8,128)}, f32[2,64,64]{1,2,0:T(8,128)S(1)}) fusion(f32[1,6,2,64,64]{3,4,2,1,0:T(8,128)} %get-tuple-element.11, bf16[2048,2,64]{0,2,1:T(8,128)(2,1)} %copy-done.6, bf16[2048,3,2,64]{0,3,2,1:T(8,128)(2,1)S(1)} %copy-done.1), kind=kOutput, calls=%fused_computation.43 | convolution fusion | flops 33562624 | bytes 1146880 | tf_op jit(solution)/shard_map/tbr,tbc->brc/dot_general | solution.py:15
  147.8 0.1 copy.80
  147.9 0.0 copy-done.3
  147.9 0.0 copy-start.4
  147.9 2.0 %bitcast_dynamic-update-slice_fusion = (f32[1,6,2,64,64]{3,4,2,1,0:T(8,128)}, f32[2,64,64]{1,2,0:T(8,128)S(1)}) fusion(f32[1,6,2,64,64]{3,4,2,1,0:T(8,128)} %get-tuple-element.13, bf16[2048,2,64]{0,2,1:T(8,128)(2,1)S(1)} %bitcast.173, bf16[2048,3,2,64]{0,3,2,1:T(8,128)(2,1)} %all_to_all.36), kind=kOutput, calls=%fused_computation.42 | convolution fusion | flops 33562624 | bytes 1146880 | tf_op jit(solution)/shard_map/tji,tjc->jic/dot_general | solution.py:15
  149.9 0.1 copy.82
  150.0 1.1 sqrt_multiply_fusion
  151.1 0.2 copy.86
  151.4 0.2 maximum_bitcast_fusion
  151.6 0.2 copy.87
  151.8 0.7 reshape.68
  152.6 20.5 %all_to_all.43 = f32[16,1,6144]{2,1,0:T(1,128)S(1)} all-to-all(f32[16,1,6144]{2,1,0:T(1,128)S(1)} %reshape.68), channel_id=1, replica_groups=mesh['dp'=16,'mp'=32] {'dp'}, dimensions={0} | all-to-all | bytes 786432 | tf_op jit(solution)/shard_map/all_to_all | solution.py:34
  173.0 0.5 broadcast.54
  173.6 1.6 reduce
  175.1 0.5 reshape.69
  175.6 0.2 reduce_sum.9
  175.9 0.7 divide_subtract_fusion
  (20 shorter events, 0.1 us)
Async XLA Ops:
  0.6 28.1 %copy-start.9 = (f32[1,6,2,64,64]{4,3,2,1,0:T(8,128)S(1)}, f32[1,6,2,64,64]{4,3,2,1,0:T(8,128)}, u32[]{:S(2)}) copy-start(f32[1,6,2,64,64]{4,3,2,1,0:T(8,128)} %param.11) | copy-start | bytes 589828
  1.5 27.4 %copy-start.5 = (bf16[2048,128]{1,0:T(8,128)(2,1)S(1)}, bf16[2048,128]{1,0:T(8,128)(2,1)}, u32[]{:S(2)}) copy-start(bf16[2048,128]{1,0:T(8,128)(2,1)} %param.6) | copy-start | bytes 1572868
  31.1 0.8 copy-start.2
  85.7 1.6 copy-start
  88.1 0.8 copy-start.8
  88.2 1.0 copy-start.7
  88.2 1.3 copy-start.6
  136.9 3.5 %copy-start.1 = (bf16[2048,3,2,64]{0,3,2,1:T(8,128)(2,1)S(1)}, bf16[2048,3,2,64]{0,3,2,1:T(8,128)(2,1)}, u32[]{:S(2)}) copy-start(bf16[2048,3,2,64]{0,3,2,1:T(8,128)(2,1)} %all_to_all.32) | copy-start | bytes 4718596
  142.5 5.4 %copy-start.3 = (bf16[2048,128]{0,1:T(8,128)(2,1)S(1)}, bf16[2048,128]{0,1:T(8,128)(2,1)}, u32[]{:S(2)}) copy-start(bf16[2048,128]{0,1:T(8,128)(2,1)} %copy-done.2) | copy-start | bytes 1572868
  147.9 3.4 %copy-start.4 = (f32[1,6,2,16,4,64]{5,4,3,2,1,0:T(4,128)S(1)}, f32[1,6,2,16,4,64]{5,4,3,2,1,0:T(4,128)}, u32[]{:S(2)}) copy-start(f32[1,6,2,16,4,64]{5,4,3,2,1,0:T(4,128)} %constant_dynamic-update-slice_fusion.5) | copy-start | bytes 589828
  173.0 2.8 %copy-start.10 = (f32[6,2,4,64]{3,2,1,0:T(4,128)S(1)}, f32[6,2,4,64]{3,2,1,0:T(4,128)}, u32[]{:S(2)}) copy-start(f32[6,2,4,64]{3,2,1,0:T(4,128)} %param.8) | copy-start | bytes 36868
  173.0 2.8 %copy-start.11 = (f32[6,2,4,64]{3,2,1,0:T(4,128)S(1)}, f32[6,2,4,64]{3,2,1,0:T(4,128)}, u32[]{:S(2)}) copy-start(f32[6,2,4,64]{3,2,1,0:T(4,128)} %param.9) | copy-start | bytes 36868
  173.0 2.8 %copy-start.12 = (f32[6,2,4,64]{3,2,1,0:T(4,128)S(1)}, f32[6,2,4,64]{3,2,1,0:T(4,128)}, u32[]{:S(2)}) copy-start(f32[6,2,4,64]{3,2,1,0:T(4,128)} %param.10) | copy-start | bytes 36868
where the time goes:
time: 177 us
  blocking collectives  138 us (78%)
  local copies, waits for them, and re-layouts  17.1 us (10%)
  matrix products  14.9 us (8%)
  other arithmetic  5.01 us (3%)
    all_to_all x1, blocking collectives, per_device(): lax.all_to_all(jnp.stack([y_left, y_right, back_outer], axis=1), 'mp', sp...  48.9 us
    all_to_all x1, blocking collectives, per_device(): lax.all_to_all(jnp.stack([outer, back_left, back_right], axis=1), 'mp', s...  42.3 us
    all_gather x1, blocking collectives, gather_rows(): full = lax.all_gather(moved, 'dp', axis=0, tiled=True)  26.8 us
    all_to_all x1, blocking collectives, scatter_rows(): got = lax.all_to_all(split, 'dp', split_axis=0, concat_axis=0, tiled=True)  20.5 us
    dot_general x15, matrix products, bdot(): return jnp.einsum(form, left, right, preferred_element_type=jnp.float32)  14.9 us
    unnamed x38, local copies, waits for them, and re-layouts  5.49 us

commit v1 on v0

--- a/solution.py
+++ b/solution.py
@@ -2,6 +2,7 @@
 import jax.numpy as jnp
 from jax import lax
 from jax.sharding import PartitionSpec as P
+from jax.lax import all_to_all, axis_size
 
 LAMBDA_SIZE = 100.0
 DELTA_DAMP = 0.001
@@ -74,12 +75,19 @@
     grad_three = bdot("tji,tjc->jic", perm_right, value_grad) * scale
     back_left = bdot("tjc,jic->tij", gate_grad, sampled[1]).astype(jnp.bfloat16)
     back_right = bdot("tjc,jic->tij", value_grad, sampled[3]).astype(jnp.bfloat16)
-    second = lax.all_to_all(
-        jnp.stack([outer, back_left, back_right], axis=1),
-        "mp",
-        split_axis=2,
-        concat_axis=3,
-        tiled=True,
+    second = jnp.concatenate(
+        all_to_all(
+            jnp.stack(
+                jnp.split(
+                    jnp.stack([outer, back_left, back_right], axis=1), axis_size("mp"), axis=2
+                ),
+                axis=0,
+            ),
+            "mp",
+            0,
+            0,
+        ),
+        3,
     )
     mixed_rows, rows_left, rows_right = (second[:, 0], second[:, 1], second[:, 2])
     grad_five = bdot("tji,tjc->jic", mixed_rows, grad_rows) * scale

time: 177 us -> 178 us (level)
    all_to_all x2 -> x0, local copies, waits for them, and re-layouts: 3.3 us -> none  [per_device(): lax.all_to_all(jnp.stack([outer, back_left, back_right], axis=1), 'mp', s...]
    slice x0 -> x1, local copies, waits for them, and re-layouts: none -> 2.3 us  [per_device(): second[:, 0]]
    unnamed x38 -> x67, local copies, waits for them, and re-layouts: 5.49 us -> 7.42 us
    reshape x0 -> x1, local copies, waits for them, and re-layouts: none -> 1.79 us  [per_device(): jnp.concatenate(all_to_all(jnp.stack(jnp.split(jnp.stack([outer, back_lef...]
where the time goes in v1:
time: 178 us; the launch traced here: 177 us
  blocking collectives  138 us (78%)
  local copies, waits for them, and re-layouts  18.3 us (10%)
  matrix products  14.1 us (8%)
  other arithmetic  5.04 us (3%)
    all_to_all x1, blocking collectives, per_device(): lax.all_to_all(jnp.stack([y_left, y_right, back_outer], axis=1), 'mp', sp...  48.9 us
    all_to_all x1, blocking collectives, per_device(): all_to_all(jnp.stack(jnp.split(jnp.stack([outer, back_left, back_right],...  42.3 us
    all_gather x1, blocking collectives, gather_rows(): full = lax.all_gather(moved, 'dp', axis=0, tiled=True)  26.8 us
    all_to_all x1, blocking collectives, scatter_rows(): got = lax.all_to_all(split, 'dp', split_axis=0, concat_axis=0, tiled=True)  20.5 us
    dot_general x15, matrix products, bdot(): return jnp.einsum(form, left, right, preferred_element_type=jnp.float32)  14.1 us
    unnamed x67, local copies, waits for them, and re-layouts  7.42 us

profile of v1, /device:TPU:1, one launch (start us, length us, event | category | flops | bytes accessed | tf_op | source)
XLA Modules:
  0.0 177.0 jit_solution(2309477394520920967)
XLA Ops:
  0.6 0.8 pad_maximum_fusion.2
  1.5 26.8 %all_gather.3 = f32[64,2,6,2,64]{4,3,2,1,0:T(2,128)S(1)} all-gather(f32[4,2,6,2,64]{4,3,2,1,0:T(2,128)S(1)} %bitcast.307), channel_id=1, replica_groups=mesh['dp'=16,'mp'=32] {'dp'}, dimensions={0}, use_global_device_ids=true | all-gather | bytes 417792 | tf_op jit(solution)/shard_map/all_gather | solution.py:26
  28.3 0.4 copy.63
  28.7 0.2 copy.64
  28.9 0.2 copy.65
  29.1 0.1 fusion.8
  29.2 0.3 fusion
  29.5 0.3 fusion.1
  29.8 1.2 copy.66
  31.1 0.3 fusion.2
  31.4 0.2 pad_maximum_fusion
  31.6 0.3 copy-done.1
  31.9 1.6 copy.68
  33.5 48.9 %all_to_all.28 = bf16[2048,3,64,2]{0,3,1,2:T(2,128)(2,1)S(1)} all-to-all(bf16[2048,3,64,2]{0,3,1,2:T(2,128)(2,1)S(1)} %copy.68), channel_id=1, replica_groups=mesh['dp'=16,'mp'=32] {'mp'}, dimensions={2} | all-to-all | bytes 3145728 | tf_op jit(solution)/shard_map/all_to_all | solution.py:58
  82.4 1.3 copy.115
  83.6 2.0 %all_to_all.22 = bf16[2048,3,2,64]{0,3,2,1:T(8,128)(2,1)} reshape(bf16[2048,3,2,32,2]{0,4,3,2,1:T(2,128)(2,1)S(1)} %bitcast.288) | data formatting | bytes 3145728 | tf_op jit(solution)/shard_map/all_to_all | solution.py:58
  85.7 1.5 convolution_bitcast_fusion
  87.2 0.3 convolution_bitcast_fusion.2
  87.5 0.6 multiply_convert_fusion.2
  88.2 0.3 fusion.3
  88.5 0.3 fusion.4
  88.8 0.1 copy-done.5
  88.9 0.2 copy-done.6
  89.2 0.1 copy-done.7
  89.3 0.3 fusion.5
  89.6 0.2 pad_maximum_fusion.1
  89.9 0.1 constant_dynamic-update-slice_fusion.30
  89.9 0.1 constant_dynamic-update-slice_fusion.29
  90.0 0.1 constant_dynamic-update-slice_fusion.28
  90.2 0.1 constant_dynamic-update-slice_fusion.25
  90.2 0.1 constant_dynamic-update-slice_fusion.24
  90.5 0.1 constant_dynamic-update-slice_fusion.20
  91.1 0.1 constant_dynamic-update-slice_fusion.10
  91.3 0.1 constant_dynamic-update-slice_fusion.6
  91.4 0.1 constant_dynamic-update-slice_fusion.5
  91.8 42.3 %all_to_all.29 = bf16[32,2048,3,2,2]{1,3,4,2,0:T(2,128)(2,1)S(1)} all-to-all(bf16[32,2048,3,2,2]{1,3,4,2,0:T(2,128)(2,1)S(1)} %constant_dynamic-update-slice_fusion), channel_id=1, replica_groups=mesh['dp'=16,'mp'=32] {'mp'}, dimensions={0} | all-to-all | bytes 3145728 | tf_op jit(solution)/shard_map/all_to_all | solution.py:79
  134.1 1.8 %copy.73 = bf16[2048,3,2,32,2]{0,2,4,3,1:T(2,128)(2,1)S(1)} copy(bf16[2048,3,2,32,2]{0,2,4,1,3:T(2,128)(2,1)S(1)} %bitcast.289) | data formatting | bytes 3145728 | tf_op jit(solution)/shard_map/reshape | solution.py:78
  135.9 2.3 %fusion.17 = (bf16[2048,1,2,64]{0,2,3,1:T(2,128)(2,1)}, bf16[2048,1,2,64]{0,2,3,1:T(2,128)(2,1)}, bf16[2048,1,2,64]{0,2,3,1:T(2,128)(2,1)S(1)}) fusion(bf16[2048,3,2,64]{0,2,3,1:T(2,128)(2,1)S(1)} %bitcast.286), kind=kLoop, calls=%fused_computation.135 | loop fusion | bytes 3145728 | tf_op jit(solution)/shard_map/slice | solution.py:92
  138.2 0.4 convolution_multiply_fusion.5
  138.6 0.1 copy.87
  138.7 0.6 constant_dynamic-update-slice_fusion.43
  139.3 2.0 %constant_dynamic-update-slice_fusion.42 = (f32[1,6,2,64,64]{3,4,2,1,0:T(8,128)}, f32[2,64,64]{1,2,0:T(8,128)S(1)}) fusion(f32[1,6,2,64,64]{3,4,2,1,0:T(8,128)} %constant_dynamic-update-slice_fusion.43, bf16[2048,2,64]{0,2,1:T(8,128)(2,1)} %copy-done.7, bf16[2048,3,2,64]{0,3,2,1:T(8,128)(2,1)S(1)} %copy-done), kind=kOutput, calls=%fused_computation.83 | convolution fusion | flops 33562624 | bytes 1146880 | tf_op jit(solution)/shard_map/tji,tjc->jic/dot_general | solution.py:16
  141.3 0.1 copy.77
  141.3 0.6 constant_dynamic-update-slice_fusion.37
  142.0 1.4 convolution_multiply_fusion.3
  143.4 0.1 copy.88
  143.5 0.6 constant_dynamic-update-slice_fusion.41
  144.1 1.9 %constant_dynamic-update-slice_fusion.40 = (f32[1,6,2,64,64]{3,4,2,1,0:T(8,128)}, f32[2,64,64]{1,2,0:T(8,128)S(1)}) fusion(f32[1,6,2,64,64]{3,4,2,1,0:T(8,128)} %constant_dynamic-update-slice_fusion.41, bf16[2048,2,64]{0,2,1:T(8,128)(2,1)} %copy-done.6, bf16[2048,3,2,64]{0,3,2,1:T(8,128)(2,1)S(1)} %copy-done), kind=kOutput, calls=%fused_computation.81 | convolution fusion | flops 33562624 | bytes 1146880 | tf_op jit(solution)/shard_map/tji,tjc->jic/dot_general | solution.py:16
  146.1 0.1 copy.81
  146.1 1.9 %constant_dynamic-update-slice_fusion.39 = (f32[1,6,2,64,64]{3,4,2,1,0:T(8,128)}, f32[2,64,64]{1,2,0:T(8,128)S(1)}) fusion(f32[1,6,2,64,64]{3,4,2,1,0:T(8,128)} %get-tuple-element.14, bf16[2048,2,64]{0,2,1:T(8,128)(2,1)} %copy-done.5, bf16[2048,3,2,64]{0,3,2,1:T(8,128)(2,1)S(1)} %copy-done), kind=kOutput, calls=%fused_computation.80 | convolution fusion | flops 33562624 | bytes 1146880 | tf_op jit(solution)/shard_map/tbr,tbc->brc/dot_general | solution.py:16
  148.1 0.1 copy.83
  148.2 2.1 %constant_dynamic-update-slice_fusion.38 = (f32[1,6,2,64,64]{3,4,2,1,0:T(8,128)}, f32[2,64,64]{1,2,0:T(8,128)S(1)}) fusion(f32[1,6,2,64,64]{3,4,2,1,0:T(8,128)} %get-tuple-element.16, bf16[2048,2,64]{0,2,1:T(8,128)(2,1)S(1)} %bitcast.297, bf16[2048,1,2,64]{0,2,3,1:T(2,128)(2,1)} %get-tuple-element.9), kind=kOutput, calls=%fused_computation.79 | convolution fusion | flops 33562624 | bytes 1146880 | tf_op jit(solution)/shard_map/tji,tjc->jic/dot_general | solution.py:16
  150.3 0.1 copy.86
  150.4 1.1 sqrt_multiply_fusion
  151.5 0.2 copy.90
  151.8 0.2 maximum_bitcast_fusion
  152.1 0.2 copy.91
  152.3 0.7 reshape.76
  153.0 20.5 %all_to_all.30 = f32[16,1,6144]{2,1,0:T(1,128)S(1)} all-to-all(f32[16,1,6144]{2,1,0:T(1,128)S(1)} %reshape.76), channel_id=1, replica_groups=mesh['dp'=16,'mp'=32] {'dp'}, dimensions={0} | all-to-all | bytes 786432 | tf_op jit(solution)/shard_map/all_to_all | solution.py:35
  173.5 0.5 broadcast.54
  174.0 1.6 reduce
  175.6 0.5 reshape.77
  176.1 0.2 reduce_sum.9
  176.3 0.7 divide_subtract_fusion
  (49 shorter events, 1.5 us)
Async XLA Ops:
  0.6 28.1 %copy-start.8 = (f32[1,6,2,64,64]{4,3,2,1,0:T(8,128)S(1)}, f32[1,6,2,64,64]{4,3,2,1,0:T(8,128)}, u32[]{:S(2)}) copy-start(f32[1,6,2,64,64]{4,3,2,1,0:T(8,128)} %param.11) | copy-start | bytes 589828
  1.5 27.4 %copy-start.4 = (bf16[2048,128]{1,0:T(8,128)(2,1)S(1)}, bf16[2048,128]{1,0:T(8,128)(2,1)}, u32[]{:S(2)}) copy-start(bf16[2048,128]{1,0:T(8,128)(2,1)} %param.6) | copy-start | bytes 1572868
  31.1 0.8 copy-start.1
  85.7 1.6 copy-start
  88.2 0.8 copy-start.5
  88.2 1.0 copy-start.6
  88.2 1.1 copy-start.7
  143.4 4.8 %copy-start.2 = (bf16[2048,128]{0,1:T(8,128)(2,1)S(1)}, bf16[2048,128]{0,1:T(8,128)(2,1)}, u32[]{:S(2)}) copy-start(bf16[2048,128]{0,1:T(8,128)(2,1)} %copy-done.1) | copy-start | bytes 1572868
  148.2 3.5 %copy-start.3 = (f32[1,6,2,16,4,64]{5,4,3,2,1,0:T(4,128)S(1)}, f32[1,6,2,16,4,64]{5,4,3,2,1,0:T(4,128)}, u32[]{:S(2)}) copy-start(f32[1,6,2,16,4,64]{5,4,3,2,1,0:T(4,128)} %constant_dynamic-update-slice_fusion.37) | copy-start | bytes 589828
  173.5 2.8 %copy-start.9 = (f32[6,2,4,64]{3,2,1,0:T(4,128)S(1)}, f32[6,2,4,64]{3,2,1,0:T(4,128)}, u32[]{:S(2)}) copy-start(f32[6,2,4,64]{3,2,1,0:T(4,128)} %param.8) | copy-start | bytes 36868
  173.5 2.8 %copy-start.10 = (f32[6,2,4,64]{3,2,1,0:T(4,128)S(1)}, f32[6,2,4,64]{3,2,1,0:T(4,128)}, u32[]{:S(2)}) copy-start(f32[6,2,4,64]{3,2,1,0:T(4,128)} %param.9) | copy-start | bytes 36868
  173.5 2.8 %copy-start.11 = (f32[6,2,4,64]{3,2,1,0:T(4,128)S(1)}, f32[6,2,4,64]{3,2,1,0:T(4,128)}, u32[]{:S(2)}) copy-start(f32[6,2,4,64]{3,2,1,0:T(4,128)} %param.10) | copy-start | bytes 36868
